TPU v7x, 32 devices: a whole 2x2x4 slice. The times are simulated.
32 devices in a mesh: groups: 2 (over x), seq: 16 (over z, y, core).
Axes of the slice: x: 2, y: 2, z: 4, core: 2. Of those that a mesh axis runs over, the one named last changes fastest.
Arguments:
- video_qkv: bfloat16 [4, 1536, 3, 4096], P('groups', 'seq'), parts along dimension 0, may hold values from -48 to 48
- video_cross_q: bfloat16 [4, 1536, 4096], P('groups', 'seq'), parts along dimension 0, may hold values from -48 to 48
- audio_kv_v: bfloat16 [4, 512, 2, 4096], P('groups', 'seq'), parts along dimension 0, may hold values from -4 to 4
- audio_qkv: bfloat16 [4, 512, 3, 2048], P('groups', 'seq'), parts along dimension 0, may hold values from -48 to 48
- audio_cross_q: bfloat16 [4, 512, 2048], P('groups', 'seq'), parts along dimension 0, may hold values from -48 to 48
- video_kv_a: bfloat16 [4, 1536, 2, 2048], P('groups', 'seq'), parts along dimension 0, may hold values from -4 to 4
- audio_valid: int32 [4], P('groups'), parts along dimension 0, may hold values from 256 to 512, as said below
- branch_prompt: int32 [4], P('groups'), parts along dimension 0, may hold values from 0 to 3
- video_gate: float32 [4, 4096], replicated, may hold values from 0.5 to 1.5
- audio_gate: float32 [4, 2048], replicated, may hold values from 0.5 to 1.5
Outputs:
- video_out: bfloat16 [4, 1536, 4096], P('groups', 'seq'), parts along dimension 0
- audio_out: bfloat16 [4, 512, 2048], P('groups', 'seq'), parts along dimension 0
There are 2 independent parts, one for each index of `groups`. A program takes and returns all parts, laid end to end along the dimension named above; an argument that names none is the same for every part. Nothing has to cross between parts.
Inputs may be any that keep to these rules, and one draw needn't show every extreme that they name: `audio_valid`: at least one branch has all 512 audio tokens valid.
All inputs are finite; a program needn't handle non-finite values.
Results may differ from a plain program's by a relative error of at most 0.0058.
Values may be sent and summed in bfloat16 or wider, within the bound.
A program may use at most 128 MiB of HBM per device.

v0:
```python
import jax
import jax.numpy as jnp
from jax import lax
from jax.sharding import PartitionSpec as P

HV = 32
HA = 16
PROMPTS = 4


def block_attend(queries, key_rows, value_rows, allowed):
    scores = jnp.dot(queries, key_rows.T, preferred_element_type=jnp.float32) * queries.shape[
        -1
    ] ** (-0.5)
    if allowed is not None:
        scores = jnp.where(allowed[None, :], scores, -jnp.inf)
    row_max = jnp.max(scores, axis=1, keepdims=True)
    weights = jnp.exp(scores - row_max)
    shares = (weights / jnp.sum(weights, axis=1, keepdims=True)).astype(jnp.bfloat16)
    return jnp.dot(shares, value_rows, preferred_element_type=jnp.float32).astype(jnp.bfloat16)


def attend(queries, key_rows, value_rows, allowed):
    row_count, head_width = queries.shape
    block_rows = row_count
    while block_rows % 2 == 0 and block_rows // 2 >= 512:
        block_rows = block_rows // 2

    def one_block(block_queries):
        return block_attend(block_queries, key_rows, value_rows, allowed)

    result = lax.map(one_block, queries.reshape(row_count // block_rows, block_rows, head_width))
    return result.reshape(row_count, head_width)


def to_items(source, head_count):
    lead_count, row_count = (source.shape[0], source.shape[1])
    middle = source.shape[2:-1]
    head_width = source.shape[-1] // head_count
    result = source.reshape((lead_count, row_count) + middle + (head_count, head_width))
    axes_order = (0, len(middle) + 2, 1) + tuple(range(2, len(middle) + 2)) + (len(middle) + 3,)
    result = jnp.transpose(result, axes_order)
    return result.reshape((lead_count * head_count, row_count) + middle + (head_width,))


def from_items(source, head_count):
    item_count, row_count, head_width = source.shape
    result = source.reshape(item_count // head_count, head_count, row_count, head_width)
    return jnp.transpose(result, (0, 2, 1, 3)).reshape(
        item_count // head_count, row_count, head_count * head_width
    )


def self_items(packed):
    return attend(packed[:, 0], packed[:, 1], packed[:, 2], None)


def self_masked(packed):
    return attend(packed[0][:, 0], packed[0][:, 1], packed[0][:, 2], packed[1] > 0.5)


def cross_masked(packed):
    return attend(packed[0], packed[1][:, 0], packed[1][:, 1], packed[2] > 0.5)


def cross_items(packed):
    return attend(packed[0], packed[1][:, 0], packed[1][:, 1], None)


def local_gates(gates, head_count, item_count):
    gate_items = to_items(gates[:, None, :], head_count)[:, 0, :]
    first_item = lax.axis_index("seq") * item_count
    return lax.dynamic_slice_in_dim(gate_items, first_item, item_count, 0)


def on_device(
    video_qkv,
    video_cross_q,
    audio_kv_v,
    audio_qkv,
    audio_cross_q,
    video_kv_a,
    audio_valid,
    branch_prompt,
    video_gate,
    audio_gate,
):
    local_audio = audio_qkv.shape[1]
    positions = lax.axis_index("seq") * local_audio + jnp.arange(local_audio, dtype=jnp.int32)
    allowed_local = (positions[None, :] < audio_valid[:, None]).astype(jnp.bfloat16)
    video_items = to_items(video_qkv, HV)
    video_query = to_items(video_cross_q, HV)
    video_keys = to_items(audio_kv_v, HV)
    video_allowed = jnp.repeat(allowed_local, HV, axis=0)
    audio_items = to_items(audio_qkv, HA)
    audio_query = to_items(audio_cross_q, HA)
    audio_keys = to_items(video_kv_a, HA)
    audio_allowed = jnp.repeat(allowed_local, HA, axis=0)
    video_items, video_query, video_keys, video_allowed = (
        lax.all_to_all(video_items, "seq", split_axis=0, concat_axis=1, tiled=True),
        lax.all_to_all(video_query, "seq", split_axis=0, concat_axis=1, tiled=True),
        lax.all_to_all(video_keys, "seq", split_axis=0, concat_axis=1, tiled=True),
        lax.all_to_all(video_allowed, "seq", split_axis=0, concat_axis=1, tiled=True),
    )
    audio_items, audio_query, audio_keys, audio_allowed = (
        lax.all_to_all(audio_items, "seq", split_axis=0, concat_axis=1, tiled=True),
        lax.all_to_all(audio_query, "seq", split_axis=0, concat_axis=1, tiled=True),
        lax.all_to_all(audio_keys, "seq", split_axis=0, concat_axis=1, tiled=True),
        lax.all_to_all(audio_allowed, "seq", split_axis=0, concat_axis=1, tiled=True),
    )
    video_self = lax.map(self_items, video_items)
    video_cross = lax.map(cross_masked, (video_query, video_keys, video_allowed))
    audio_self = lax.map(self_masked, (audio_items, audio_allowed))
    audio_cross = lax.map(cross_items, (audio_query, audio_keys))
    chosen = (branch_prompt[:, None] == jnp.arange(PROMPTS, dtype=jnp.int32)[None, :]).astype(
        jnp.float32
    )
    video_gates = jnp.dot(chosen, video_gate, precision=lax.Precision.HIGHEST)
    audio_gates = jnp.dot(chosen, audio_gate, precision=lax.Precision.HIGHEST)
    video_slice = local_gates(video_gates, HV, video_self.shape[0])
    audio_slice = local_gates(audio_gates, HA, audio_self.shape[0])
    video_return = (
        video_self.astype(jnp.float32) + video_slice[:, None, :] * video_cross.astype(jnp.float32)
    ).astype(jnp.bfloat16)
    audio_return = (
        audio_self.astype(jnp.float32) + audio_slice[:, None, :] * audio_cross.astype(jnp.float32)
    ).astype(jnp.bfloat16)
    video_back, audio_back = (
        lax.all_to_all(video_return, "seq", split_axis=1, concat_axis=0, tiled=True),
        lax.all_to_all(audio_return, "seq", split_axis=1, concat_axis=0, tiled=True),
    )
    return (from_items(video_back, HV), from_items(audio_back, HA))


def solution(mesh):
    placed = (
        P("groups", "seq", None, None),
        P("groups", "seq", None),
        P("groups", "seq", None, None),
        P("groups", "seq", None, None),
        P("groups", "seq", None),
        P("groups", "seq", None, None),
        P("groups"),
        P("groups"),
        P(),
        P(),
    )
    return jax.shard_map(
        on_device,
        mesh=mesh,
        in_specs=placed,
        out_specs=(P("groups", "seq", None), P("groups", "seq", None)),
        check_vma=False,
    )
```

profile of v0, /device:TPU:13, one launch (start us, length us, event | category | flops | bytes accessed | tf_op | source)
XLA Modules:
  0.0 380.2 jit_solution(1439106227688947911)
XLA Ops:
  2.1 6.6 %all-to-all-start.5 = ((bf16[16,2,32]{2,1,0:T(2,128)(2,1)}), bf16[16,2,32]{2,1,0:T(2,128)(2,1)S(1)}, u32[]{:S(2)}, u32[]{:S(2)}) async-start(bf16[16,2,32]{2,1,0:T(2,128)(2,1)} %broadcast_in_dim.90), calls=%async_computation.5 | async-start | bytes 16384 | tf_op jit(solution)/shard_map/all_to_all | solution.py:109
  8.6 1.0 copy.113
  9.6 2.7 all-to-all-done.5
  13.0 6.0 %all-to-all-start.3 = ((bf16[16,4,32]{2,1,0:T(4,128)(2,1)}), bf16[16,4,32]{2,1,0:T(4,128)(2,1)S(1)}, u32[]{:S(2)}, u32[]{:S(2)}) async-start(bf16[16,4,32]{2,1,0:T(4,128)(2,1)} %broadcast_in_dim.89), calls=%async_computation.3 | async-start | bytes 32768 | tf_op jit(solution)/shard_map/all_to_all | solution.py:103
  19.8 3.4 all-to-all-done.3
  23.2 5.8 %all-to-all-start.7 = ((bf16[32,32,128]{2,1,0:T(8,128)(2,1)}), bf16[32,32,128]{2,1,0:T(8,128)(2,1)S(1)}, u32[]{:S(2)}, u32[]{:S(2)}) async-start(bf16[32,32,128]{2,1,0:T(8,128)(2,1)} %bitcast.53), calls=%async_computation.7 | async-start | bytes 524288 | tf_op jit(solution)/shard_map/all_to_all | solution.py:107
  29.2 1.1 copy.93
  30.3 6.7 %all-to-all-done.7 = bf16[32,32,128]{2,1,0:T(8,128)(2,1)S(1)} async-done(((bf16[32,32,128]{2,1,0:T(8,128)(2,1)}), bf16[32,32,128]{2,1,0:T(8,128)(2,1)S(1)}, u32[]{:S(2)}, u32[]{:S(2)}) %all-to-all-start.7) | async-done | bytes 262176 | tf_op jit(solution)/shard_map/all_to_all | solution.py:107
  37.7 5.6 %all-to-all-start.6 = ((bf16[32,32,3,128]{3,1,2,0:T(8,128)(2,1)}), bf16[32,32,3,128]{3,1,2,0:T(8,128)(2,1)S(1)}, u32[]{:S(2)}, u32[]{:S(2)}) async-start(bf16[32,32,3,128]{3,1,2,0:T(8,128)(2,1)} %bitcast.48), calls=%async_computation.6 | async-start | bytes 1572864 | tf_op jit(solution)/shard_map/all_to_all | solution.py:106
  44.2 1.7 copy.85
  45.8 16.8 %all-to-all-done.6 = bf16[32,32,3,128]{3,1,2,0:T(8,128)(2,1)S(1)} async-done(((bf16[32,32,3,128]{3,1,2,0:T(8,128)(2,1)}), bf16[32,32,3,128]{3,1,2,0:T(8,128)(2,1)S(1)}, u32[]{:S(2)}, u32[]{:S(2)}) %all-to-all-start.6) | async-done | bytes 786464 | tf_op jit(solution)/shard_map/all_to_all | solution.py:106
  62.6 4.9 %all-to-all-start.2 = ((bf16[64,32,2,128]{3,1,2,0:T(8,128)(2,1)}), bf16[64,32,2,128]{3,1,2,0:T(8,128)(2,1)S(1)}, u32[]{:S(2)}, u32[]{:S(2)}) async-start(bf16[64,32,2,128]{3,1,2,0:T(8,128)(2,1)} %bitcast.36), calls=%async_computation.2 | async-start | bytes 2097152 | tf_op jit(solution)/shard_map/all_to_all | solution.py:102
  68.2 1.8 copy.82
  69.9 22.5 %all-to-all-done.2 = bf16[64,32,2,128]{3,1,2,0:T(8,128)(2,1)S(1)} async-done(((bf16[64,32,2,128]{3,1,2,0:T(8,128)(2,1)}), bf16[64,32,2,128]{3,1,2,0:T(8,128)(2,1)S(1)}, u32[]{:S(2)}, u32[]{:S(2)}) %all-to-all-start.2) | async-done | bytes 1048608 | tf_op jit(solution)/shard_map/all_to_all | solution.py:102
  92.4 1.0 copy-done.4
  93.4 4.9 %all-to-all-start.1 = ((bf16[64,96,128]{2,1,0:T(8,128)(2,1)}), bf16[64,96,128]{2,1,0:T(8,128)(2,1)S(1)}, u32[]{:S(2)}, u32[]{:S(2)}) async-start(bf16[64,96,128]{2,1,0:T(8,128)(2,1)} %bitcast.30), calls=%async_computation.1 | async-start | bytes 3145728 | tf_op jit(solution)/shard_map/all_to_all | solution.py:101
  98.3 2.8 reshape.114
  101.1 1.8 copy.98
  102.9 31.6 %all-to-all-done.1 = bf16[64,96,128]{2,1,0:T(8,128)(2,1)S(1)} async-done(((bf16[64,96,128]{2,1,0:T(8,128)(2,1)}), bf16[64,96,128]{2,1,0:T(8,128)(2,1)S(1)}, u32[]{:S(2)}, u32[]{:S(2)}) %all-to-all-start.1) | async-done | bytes 1572896 | tf_op jit(solution)/shard_map/all_to_all | solution.py:101
  134.5 1.1 copy-done.2
  135.6 4.9 %all-to-all-start.8 = ((bf16[32,96,2,128]{3,1,2,0:T(8,128)(2,1)}), bf16[32,96,2,128]{3,1,2,0:T(8,128)(2,1)}, u32[]{:S(2)}, u32[]{:S(2)}) async-start(bf16[32,96,2,128]{3,1,2,0:T(8,128)(2,1)} %bitcast.59), calls=%async_computation.8 | async-start | bytes 3145728 | tf_op jit(solution)/shard_map/all_to_all | solution.py:108
  140.6 3.8 copy.110
  144.4 4.0 %copy.80 = bf16[2,32,96,3,128]{4,2,3,1,0:T(8,128)(2,1)} copy(bf16[2,32,96,3,128]{4,1,2,3,0:T(8,128)(2,1)S(1)} %bitcast.231) | data formatting | bytes 9437184 | tf_op jit(solution)/shard_map/transpose | solution.py:42
  149.9 2.1 while.72
  152.0 1.1 copy.86
  154.0 22.8 %all-to-all-done.8 = bf16[32,96,2,128]{3,1,2,0:T(8,128)(2,1)} async-done(((bf16[32,96,2,128]{3,1,2,0:T(8,128)(2,1)}), bf16[32,96,2,128]{3,1,2,0:T(8,128)(2,1)}, u32[]{:S(2)}, u32[]{:S(2)}) %all-to-all-start.8) | async-done | bytes 1572896 | tf_op jit(solution)/shard_map/all_to_all | solution.py:108
  176.8 4.9 %all-to-all-start = ((bf16[64,96,3,128]{3,1,2,0:T(8,128)(2,1)}), bf16[64,96,3,128]{3,1,2,0:T(8,128)(2,1)}, u32[]{:S(2)}, u32[]{:S(2)}) async-start(bf16[64,96,3,128]{3,1,2,0:T(8,128)(2,1)} %bitcast.230), calls=%async_computation | async-start | bytes 9437184 | tf_op jit(solution)/shard_map/all_to_all | solution.py:100
  181.8 1.5 copy.99
  184.0 6.3 %while.73 = (s32[]{:T(128)}, bf16[2,512,128]{2,1,0:T(8,128)(2,1)}, bf16[2,512,128]{2,1,0:T(8,128)(2,1)S(1)}, bf16[2,1536,2,128]{3,1,2,0:T(8,128)(2,1)S(1)}, s32[]{:T(128)}) while((s32[]{:T(128)}, bf16[2,512,128]{2,1,0:T(8,128)(2,1)}, bf16[2,512,128]{2,1,0:T(8,128)(2,1)S(1)}, bf16[2,1536,2,128]{3,1,2,0:T(8,128)(2,1)S(1)}, s32[]{:T(128)}) %tuple.140), condition=%wide.region_19.20_spmd, body=%wide.region_16.19_spmd.sunk | while | flops 408222720 | bytes 14166153 | solution.py:114
  190.3 1.1 add_convert_fusion.1
  192.4 1.3 broadcast.58.clone
  193.8 17.0 %while.71 = (s32[]{:T(128)}, bf16[4,1536,128]{2,1,0:T(8,128)(2,1)}, bf16[4,1536,128]{2,1,0:T(8,128)(2,1)S(1)}, bf16[4,512,2,128]{3,1,2,0:T(8,128)(2,1)}, bf16[4,...) while((s32[]{:T(128)}, bf16[4,1536,128]{2,1,0:T(8,128)(2,1)}, ...), condition=%wide.region_11.12_spmd, body=%wide.region_6.11_spmd.sunk | while | flops 204570624 | bytes 8015114 | solution.py:112
  193.8 1.0 dynamic-slice_bitcast_fusion.9
  194.8 2.4 while.75
  198.1 1.0 dynamic-slice_bitcast_fusion.9
  199.1 2.4 while.75
  203.3 2.4 while.75
  207.6 2.4 while.75
  210.7 74.7 %all-to-all-done = bf16[64,96,3,128]{3,1,2,0:T(8,128)(2,1)} async-done(((bf16[64,96,3,128]{3,1,2,0:T(8,128)(2,1)}), bf16[64,96,3,128]{3,1,2,0:T(8,128)(2,1)}, u32[]{:S(2)}, u32[]{:S(2)}) %all-to-all-start) | async-done | bytes 4718624 | tf_op jit(solution)/shard_map/all_to_all | solution.py:100
  285.5 4.9 %all-to-all-start.9 = ((bf16[2,512,128]{2,0,1:T(2,128)(2,1)}), bf16[2,512,128]{2,0,1:T(2,128)(2,1)}, u32[]{:S(2)}, u32[]{:S(2)}) async-start(bf16[2,512,128]{2,0,1:T(2,128)(2,1)} %copy.100), calls=%async_computation.9 | async-start | bytes 524288 | tf_op jit(solution)/shard_map/all_to_all | solution.py:130
  290.4 5.6 %copy.81 = bf16[4,16,96,3,128]{4,2,1,3,0:T(8,128)(2,1)} copy(bf16[4,16,96,3,128]{4,2,3,0,1:T(8,128)(2,1)} %bitcast.27) | data formatting | bytes 9437184 | tf_op jit(solution)/shard_map/all_to_all | solution.py:100
  296.2 29.7 %while.69 = (s32[]{:T(128)}, bf16[4,1536,128]{2,1,0:T(8,128)(2,1)S(1)}, bf16[4,1536,3,128]{3,1,2,0:T(8,128)(2,1)}, s32[]{:T(128)}, s32[]{:T(128)}, /*index=5*/s32[]{:T(128)}) while((s32[]{:T(128)}, bf16[4,1536,128]{2,1,0:T(8,128)(2,1)S(1)}, bf16[4,1536,3,128]{3,1,2,0:T(8,128)(2,1)}, s32[]{:T(128)}, s32[]{:T(128)}, /*index=5*/s32[]{:T(128)}) %tuple.136), condition=%wide.region_5.6_spmd, body=%wide.region_0.5_spmd.sunk | while | flops 614693376 | bytes 20858080 | solution.py:111
  296.2 1.4 dynamic-slice_bitcast_fusion.8
  297.6 5.9 %while.74 = (s32[]{:T(128)}, bf16[2,768,128]{2,1,0:T(8,128)(2,1)S(1)}, bf16[2,768,128]{2,1,0:T(8,128)(2,1)S(1)}, bf16[1536,128]{1,0:T(8,128)(2,1)S(1)}, bf16[1536,128]{1,0:T(8,128)(2,1)S(1)}, /*index=5*/s32[]{:T(128)}) while((s32[]{:T(128)}, bf16[2,768,128]{2,1,0:T(8,128)(2,1)S(1)}, bf16[2,768,128]{2,1,0:T(8,128)(2,1)S(1)}, ...), condition=%wide.region_4.4_spmd, body=%wide.region_1.3_spmd.sunk | while | flops 614693376 | bytes 15352917 | solution.py:32
  299.4 1.2 fusion.70
  302.3 1.2 fusion.70
  303.6 1.4 dynamic-slice_bitcast_fusion.8
  305.1 5.9 %while.74 = (s32[]{:T(128)}, bf16[2,768,128]{2,1,0:T(8,128)(2,1)S(1)}, bf16[2,768,128]{2,1,0:T(8,128)(2,1)S(1)}, bf16[1536,128]{1,0:T(8,128)(2,1)S(1)}, bf16[1536,128]{1,0:T(8,128)(2,1)S(1)}, /*index=5*/s32[]{:T(128)}) while((s32[]{:T(128)}, bf16[2,768,128]{2,1,0:T(8,128)(2,1)S(1)}, bf16[2,768,128]{2,1,0:T(8,128)(2,1)S(1)}, ...), condition=%wide.region_4.4_spmd, body=%wide.region_1.3_spmd.sunk | while | flops 614693376 | bytes 15352917 | solution.py:32
  306.8 1.2 fusion.70
  309.8 1.2 fusion.70
  311.0 1.4 dynamic-slice_bitcast_fusion.8
  312.5 5.9 %while.74 = (s32[]{:T(128)}, bf16[2,768,128]{2,1,0:T(8,128)(2,1)S(1)}, bf16[2,768,128]{2,1,0:T(8,128)(2,1)S(1)}, bf16[1536,128]{1,0:T(8,128)(2,1)S(1)}, bf16[1536,128]{1,0:T(8,128)(2,1)S(1)}, /*index=5*/s32[]{:T(128)}) while((s32[]{:T(128)}, bf16[2,768,128]{2,1,0:T(8,128)(2,1)S(1)}, bf16[2,768,128]{2,1,0:T(8,128)(2,1)S(1)}, ...), condition=%wide.region_4.4_spmd, body=%wide.region_1.3_spmd.sunk | while | flops 614693376 | bytes 15352917 | solution.py:32
  314.3 1.2 fusion.70
  317.2 1.2 fusion.70
  318.5 1.4 dynamic-slice_bitcast_fusion.8
  319.9 5.9 %while.74 = (s32[]{:T(128)}, bf16[2,768,128]{2,1,0:T(8,128)(2,1)S(1)}, bf16[2,768,128]{2,1,0:T(8,128)(2,1)S(1)}, bf16[1536,128]{1,0:T(8,128)(2,1)S(1)}, bf16[1536,128]{1,0:T(8,128)(2,1)S(1)}, /*index=5*/s32[]{:T(128)}) while((s32[]{:T(128)}, bf16[2,768,128]{2,1,0:T(8,128)(2,1)S(1)}, bf16[2,768,128]{2,1,0:T(8,128)(2,1)S(1)}, ...), condition=%wide.region_4.4_spmd, body=%wide.region_1.3_spmd.sunk | while | flops 614693376 | bytes 15352917 | solution.py:32
  321.7 1.2 fusion.70
  324.6 1.2 fusion.70
  325.9 1.9 add_convert_fusion
  327.8 8.2 %copy.88 = bf16[4,1536,128]{2,0,1:T(4,128)(2,1)} copy(bf16[4,1536,128]{2,1,0:T(8,128)(2,1)S(1)} %add_convert_fusion) | data formatting | bytes 3145728 | tf_op jit(solution)/shard_map/convert_element_type | solution.py:124
  336.0 6.0 %all-to-all-start.4 = ((bf16[4,1536,128]{2,0,1:T(4,128)(2,1)}), bf16[4,1536,128]{2,0,1:T(4,128)(2,1)S(1)}, u32[]{:S(2)}, u32[]{:S(2)}) async-start(bf16[4,1536,128]{2,0,1:T(4,128)(2,1)} %copy.88), calls=%async_computation.4 | async-start | bytes 3145728 | tf_op jit(solution)/shard_map/all_to_all | solution.py:129
  342.0 1.0 copy.101
  343.8 34.4 %all-to-all-done.4 = bf16[4,1536,128]{2,0,1:T(4,128)(2,1)S(1)} async-done(((bf16[4,1536,128]{2,0,1:T(4,128)(2,1)}), bf16[4,1536,128]{2,0,1:T(4,128)(2,1)S(1)}, u32[]{:S(2)}, u32[]{:S(2)}) %all-to-all-start.4) | async-done | bytes 1572896 | tf_op jit(solution)/shard_map/all_to_all | solution.py:129
  378.6 1.6 copy.116
  (165 shorter events, 48.2 us)
Async XLA Ops:
  0.6 147.7 %copy-start = (f32[4,4096]{1,0:T(4,128)S(1)}, f32[4,4096]{1,0:T(4,128)}, u32[]{:S(2)}) copy-start(f32[4,4096]{1,0:T(4,128)} %param.30) | copy-start | bytes 196612
  0.6 28.4 %copy-start.15 = (bf16[2,32,3,2048]{3,1,2,0:T(8,128)(2,1)S(1)}, bf16[2,32,3,2048]{3,1,2,0:T(8,128)(2,1)}, u32[]{:S(2)}) copy-start(bf16[2,32,3,2048]{3,1,2,0:T(8,128)(2,1)} %param.25) | copy-start | bytes 2359300
  2.1 10.3 %all-to-all-start.5 = ((bf16[16,2,32]{2,1,0:T(2,128)(2,1)}), bf16[16,2,32]{2,1,0:T(2,128)(2,1)S(1)}, u32[]{:S(2)}, u32[]{:S(2)}) async-start(bf16[16,2,32]{2,1,0:T(2,128)(2,1)} %broadcast_in_dim.90), calls=%async_computation.5 | async-start | bytes 16384 | tf_op jit(solution)/shard_map/all_to_all | solution.py:109
  13.0 10.2 %all-to-all-start.3 = ((bf16[16,4,32]{2,1,0:T(4,128)(2,1)}), bf16[16,4,32]{2,1,0:T(4,128)(2,1)S(1)}, u32[]{:S(2)}, u32[]{:S(2)}) async-start(bf16[16,4,32]{2,1,0:T(4,128)(2,1)} %broadcast_in_dim.89), calls=%async_computation.3 | async-start | bytes 32768 | tf_op jit(solution)/shard_map/all_to_all | solution.py:103
  23.2 13.8 %all-to-all-start.7 = ((bf16[32,32,128]{2,1,0:T(8,128)(2,1)}), bf16[32,32,128]{2,1,0:T(8,128)(2,1)S(1)}, u32[]{:S(2)}, u32[]{:S(2)}) async-start(bf16[32,32,128]{2,1,0:T(8,128)(2,1)} %bitcast.53), calls=%async_computation.7 | async-start | bytes 524288 | tf_op jit(solution)/shard_map/all_to_all | solution.py:107
  29.2 14.2 %copy-start.9 = (bf16[2,32,2,4096]{3,2,1,0:T(2,128)(2,1)S(1)}, bf16[2,32,2,4096]{3,2,1,0:T(2,128)(2,1)}, u32[]{:S(2)}) copy-start(bf16[2,32,2,4096]{3,2,1,0:T(2,128)(2,1)} %param.24) | copy-start | bytes 3145732
  37.0 0.7 copy-start.10
  37.7 24.9 %all-to-all-start.6 = ((bf16[32,32,3,128]{3,1,2,0:T(8,128)(2,1)}), bf16[32,32,3,128]{3,1,2,0:T(8,128)(2,1)S(1)}, u32[]{:S(2)}, u32[]{:S(2)}) async-start(bf16[32,32,3,128]{3,1,2,0:T(8,128)(2,1)} %bitcast.48), calls=%async_computation.6 | async-start | bytes 1572864 | tf_op jit(solution)/shard_map/all_to_all | solution.py:106
  45.8 21.7 %copy-start.8 = (bf16[2,96,4096]{2,1,0:T(8,128)(2,1)S(1)}, bf16[2,96,4096]{2,1,0:T(8,128)(2,1)}, u32[]{:S(2)}) copy-start(bf16[2,96,4096]{2,1,0:T(8,128)(2,1)} %param.23) | copy-start | bytes 4718596
  62.6 5.3 %copy-start.6 = (bf16[32,32,3,128]{3,1,2,0:T(8,128)(2,1)}, bf16[32,32,3,128]{3,1,2,0:T(8,128)(2,1)S(1)}, u32[]{:S(2)}) copy-start(bf16[32,32,3,128]{3,1,2,0:T(8,128)(2,1)S(1)} %all-to-all-done.6) | copy-start | bytes 2359300
  62.6 29.8 %all-to-all-start.2 = ((bf16[64,32,2,128]{3,1,2,0:T(8,128)(2,1)}), bf16[64,32,2,128]{3,1,2,0:T(8,128)(2,1)S(1)}, u32[]{:S(2)}, u32[]{:S(2)}) async-start(bf16[64,32,2,128]{3,1,2,0:T(8,128)(2,1)} %bitcast.36), calls=%async_computation.2 | async-start | bytes 2097152 | tf_op jit(solution)/shard_map/all_to_all | solution.py:102
  92.4 1.0 copy-start.4
  93.4 41.1 %all-to-all-start.1 = ((bf16[64,96,128]{2,1,0:T(8,128)(2,1)}), bf16[64,96,128]{2,1,0:T(8,128)(2,1)S(1)}, u32[]{:S(2)}, u32[]{:S(2)}) async-start(bf16[64,96,128]{2,1,0:T(8,128)(2,1)} %bitcast.30), calls=%async_computation.1 | async-start | bytes 3145728 | tf_op jit(solution)/shard_map/all_to_all | solution.py:101
  134.5 1.1 copy-start.2
  135.6 41.2 %all-to-all-start.8 = ((bf16[32,96,2,128]{3,1,2,0:T(8,128)(2,1)}), bf16[32,96,2,128]{3,1,2,0:T(8,128)(2,1)}, u32[]{:S(2)}, u32[]{:S(2)}) async-start(bf16[32,96,2,128]{3,1,2,0:T(8,128)(2,1)} %bitcast.59), calls=%async_computation.8 | async-start | bytes 3145728 | tf_op jit(solution)/shard_map/all_to_all | solution.py:108
  144.3 4.0 %copy-start.17 = (s32[2]{0:T(128)S(1)}, s32[2]{0:T(128)}, u32[]{:S(2)}) copy-start(s32[2]{0:T(128)} %param.29) | copy-start | bytes 28
  144.4 4.3 %copy-start.18 = (f32[4,2048]{1,0:T(4,128)S(1)}, f32[4,2048]{1,0:T(4,128)}, u32[]{:S(2)}) copy-start(f32[4,2048]{1,0:T(4,128)} %param.31) | copy-start | bytes 98308
  144.4 5.4 %copy-start.11 = (bf16[32,32,128]{2,1,0:T(8,128)(2,1)S(1)}, bf16[32,32,128]{2,1,0:T(8,128)(2,1)}, u32[]{:S(2)}) copy-start(bf16[32,32,128]{2,1,0:T(8,128)(2,1)} %copy-done.10) | copy-start | bytes 786436
  144.4 5.4 %copy-start.7 = (bf16[32,32,3,128]{3,1,2,0:T(8,128)(2,1)S(1)}, bf16[32,32,3,128]{3,1,2,0:T(8,128)(2,1)}, u32[]{:S(2)}) copy-start(bf16[32,32,3,128]{3,1,2,0:T(8,128)(2,1)} %copy-done.6) | copy-start | bytes 2359300
  149.9 2.1 copy-start.5
  152.0 2.0 copy-start.12
  152.0 1.9 copy-start.3
  176.8 108.6 %all-to-all-start = ((bf16[64,96,3,128]{3,1,2,0:T(8,128)(2,1)}), bf16[64,96,3,128]{3,1,2,0:T(8,128)(2,1)}, u32[]{:S(2)}, u32[]{:S(2)}) async-start(bf16[64,96,3,128]{3,1,2,0:T(8,128)(2,1)} %bitcast.230), calls=%async_computation | async-start | bytes 9437184 | tf_op jit(solution)/shard_map/all_to_all | solution.py:100
  184.8 1.0 copy-start.13
  186.5 0.7 copy-start.14
  187.9 1.0 copy-start.13
  189.6 0.7 copy-start.14
  285.5 50.6 %all-to-all-start.9 = ((bf16[2,512,128]{2,0,1:T(2,128)(2,1)}), bf16[2,512,128]{2,0,1:T(2,128)(2,1)}, u32[]{:S(2)}, u32[]{:S(2)}) async-start(bf16[2,512,128]{2,0,1:T(2,128)(2,1)} %copy.100), calls=%async_computation.9 | async-start | bytes 524288 | tf_op jit(solution)/shard_map/all_to_all | solution.py:130
  296.2 29.7 %copy-start.16 = (f32[4,128]{1,0:T(4,128)S(1)}, f32[4,128]{1,0:T(4,128)}, u32[]{:S(2)}) copy-start(f32[4,128]{1,0:T(4,128)} %constant_dynamic-slice_fusion.2) | copy-start | bytes 6148
  336.0 42.2 %all-to-all-start.4 = ((bf16[4,1536,128]{2,0,1:T(4,128)(2,1)}), bf16[4,1536,128]{2,0,1:T(4,128)(2,1)S(1)}, u32[]{:S(2)}, u32[]{:S(2)}) async-start(bf16[4,1536,128]{2,0,1:T(4,128)(2,1)} %copy.88), calls=%async_computation.4 | async-start | bytes 3145728 | tf_op jit(solution)/shard_map/all_to_all | solution.py:129
  378.6 1.6 copy-start.1
where the time goes:
time: 382 us; the launch traced here: 380 us
  waiting for transfers between devices  216 us (57%)
  local copies, waits for them, and re-layouts  65 us (17%)
  starting transfers between devices  54.7 us (14%)
  matrix products  28.3 us (7%)
  other arithmetic  14.8 us (4%)
    all_to_all x1, waiting for transfers between devices, on_device(): lax.all_to_all(video_items, 'seq', split_axis=0, concat_axis=1, tiled=True)  74.7 us
    all_to_all x1, waiting for transfers between devices, on_device(): lax.all_to_all(video_return, 'seq', split_axis=1, concat_axis=0, tiled=True)  34.4 us
    all_to_all x1, waiting for transfers between devices, on_device(): lax.all_to_all(video_query, 'seq', split_axis=0, concat_axis=1, tiled=True)  31.6 us
    all_to_all x1, waiting for transfers between devices, on_device(): lax.all_to_all(audio_keys, 'seq', split_axis=0, concat_axis=1, tiled=True)  22.8 us
    all_to_all x1, waiting for transfers between devices, on_device(): lax.all_to_all(video_keys, 'seq', split_axis=0, concat_axis=1, tiled=True)  22.5 us
    all_to_all x1, waiting for transfers between devices, on_device(): lax.all_to_all(audio_items, 'seq', split_axis=0, concat_axis=1, tiled=True)  16.8 us
    dot_general x20, matrix products, block_attend(): jnp.dot(shares, value_rows, preferred_element_type=jnp.float32)  16 us
    dot_general x20, matrix products, block_attend(): jnp.dot(queries, key_rows.T, preferred_element_type=jnp.float32)  11.8 us
  transfers between devices with their start and end apart: 10, of which 9 were waited for; matrix products, arithmetic and copies ran while one was open for 26% of the time, Pallas kernels for 0%

commit v1 on v0

--- a/solution.py
+++ b/solution.py
@@ -6,6 +6,29 @@
 HV = 32
 HA = 16
 PROMPTS = 4
+
+
+def cut_along(array, dim, size):
+    shape = array.shape
+    pieces = array.reshape(*shape[:dim], size, shape[dim] // size, *shape[dim + 1 :])
+    return jnp.moveaxis(pieces, dim, 0)
+
+
+def laid_out(blocks, dim):
+    lengths = list(blocks.shape[1:])
+    lengths[dim] *= blocks.shape[0]
+    return jnp.moveaxis(blocks, 0, dim).reshape(lengths)
+
+
+def swapped_with_each(value, axis, split_dim, concat_dim):
+    length, index = (lax.axis_size(axis), lax.axis_index(axis))
+    tiles = cut_along(value, split_dim, length)
+    done = [tiles[index]]
+    for step in range(1, length):
+        sent = tiles[index ^ step]
+        done.append(lax.ppermute(sent, axis, [(i, i ^ step) for i in range(length)]))
+    tiles = jnp.stack(done)[index ^ jnp.arange(length)]
+    return laid_out(tiles, concat_dim)
 
 
 def block_attend(queries, key_rows, value_rows, allowed):
@@ -105,7 +128,7 @@
     audio_items, audio_query, audio_keys, audio_allowed = (
         lax.all_to_all(audio_items, "seq", split_axis=0, concat_axis=1, tiled=True),
         lax.all_to_all(audio_query, "seq", split_axis=0, concat_axis=1, tiled=True),
-        lax.all_to_all(audio_keys, "seq", split_axis=0, concat_axis=1, tiled=True),
+        swapped_with_each(audio_keys, "seq", 0, 1),
         lax.all_to_all(audio_allowed, "seq", split_axis=0, concat_axis=1, tiled=True),
     )
     video_self = lax.map(self_items, video_items)

time: 382 us -> 386 us (1.010)
  waiting for transfers between devices: 216 us -> 188 us
  starting transfers between devices: 54.7 us -> 76.6 us
  local copies, waits for them, and re-layouts: 65 us -> 75.5 us
    ppermute x0 -> x15, waiting for transfers between devices: none -> 37.5 us  [swapped_with_each(): lax.ppermute(sent, axis, [(i, i ^ step) for i in range(length)])]
    all_to_all x1 -> x0, waiting for transfers between devices: 22.8 us -> none  [on_device(): lax.all_to_all(audio_keys, 'seq', split_axis=0, concat_axis=1, tiled=True)]
    all_to_all x1, waiting for transfers between devices: 22.5 us -> 0.01 us  [on_device(): lax.all_to_all(video_keys, 'seq', split_axis=0, concat_axis=1, tiled=True)]
    ppermute x0 -> x15, starting transfers between devices: none -> 19.5 us  [swapped_with_each(): lax.ppermute(sent, axis, [(i, i ^ step) for i in range(length)])]
    all_to_all x1, waiting for transfers between devices: 16.8 us -> 0.5 us  [on_device(): lax.all_to_all(audio_items, 'seq', split_axis=0, concat_axis=1, tiled=True)]
    all_to_all x1, waiting for transfers between devices: 74.7 us -> 85.3 us  [on_device(): lax.all_to_all(video_items, 'seq', split_axis=0, concat_axis=1, tiled=True)]
    all_to_all x1, waiting for transfers between devices: 31.6 us -> 22.4 us  [on_device(): lax.all_to_all(video_query, 'seq', split_axis=0, concat_axis=1, tiled=True)]
    all_to_all x1, starting transfers between devices: 4.93 us -> 12.7 us  [on_device(): lax.all_to_all(video_keys, 'seq', split_axis=0, concat_axis=1, tiled=True)]
  transfers between devices with their start and end apart: 10 -> 24, of which waited for: 9 -> 11; matrix products, arithmetic and copies ran while one was open for 26% -> 28% of each run, Pallas kernels for 0% -> 0%
where the time goes in v1:
time: 386 us; the launch traced here: 384 us
  waiting for transfers between devices  188 us (49%)
  starting transfers between devices  76.6 us (20%)
  local copies, waits for them, and re-layouts  75.5 us (20%)
  matrix products  28.3 us (7%)
  other arithmetic  13.1 us (3%)
    all_to_all x1, waiting for transfers between devices, on_device(): lax.all_to_all(video_items, 'seq', split_axis=0, concat_axis=1, tiled=True)  85.3 us
    ppermute x15, waiting for transfers between devices, swapped_with_each(): lax.ppermute(sent, axis, [(i, i ^ step) for i in range(length)])  37.5 us
    all_to_all x1, waiting for transfers between devices, on_device(): lax.all_to_all(video_return, 'seq', split_axis=1, concat_axis=0, tiled=True)  34.4 us
    all_to_all x1, waiting for transfers between devices, on_device(): lax.all_to_all(video_query, 'seq', split_axis=0, concat_axis=1, tiled=True)  22.4 us
    ppermute x15, starting transfers between devices, swapped_with_each(): lax.ppermute(sent, axis, [(i, i ^ step) for i in range(length)])  19.5 us
    unnamed x58, local copies, waits for them, and re-layouts  16.4 us
    dot_general x20, matrix products, block_attend(): jnp.dot(shares, value_rows, preferred_element_type=jnp.float32)  15.9 us
    all_to_all x1, starting transfers between devices, on_device(): lax.all_to_all(video_keys, 'seq', split_axis=0, concat_axis=1, tiled=True)  12.7 us
  transfers between devices with their start and end apart: 24, of which 11 were waited for; matrix products, arithmetic and copies ran while one was open for 28% of the time, Pallas kernels for 0%

profile of v1, /device:TPU:13, one launch (start us, length us, event | category | flops | bytes accessed | tf_op | source)
XLA Modules:
  0.0 383.7 jit_solution(12361532788773907750)
XLA Ops:
  0.7 2.8 reshape.138
  4.2 1.3 dynamic-slice_bitcast_fusion.4
  6.5 1.4 collective-permute-start.2
  8.1 1.7 collective-permute-start.4
  10.4 6.0 %all-to-all-start.5 = ((bf16[16,2,32]{2,1,0:T(2,128)(2,1)}), bf16[16,2,32]{2,1,0:T(2,128)(2,1)S(1)}, u32[]{:S(2)}, u32[]{:S(2)}) async-start(bf16[16,2,32]{2,1,0:T(2,128)(2,1)} %broadcast_in_dim.91), calls=%async_computation.5 | async-start | bytes 16384 | tf_op jit(solution)/shard_map/all_to_all | solution.py:132
  16.4 1.7 copy.111
  20.7 6.0 %all-to-all-start.3 = ((bf16[16,4,32]{2,1,0:T(4,128)(2,1)}), bf16[16,4,32]{2,1,0:T(4,128)(2,1)S(1)}, u32[]{:S(2)}, u32[]{:S(2)}) async-start(bf16[16,4,32]{2,1,0:T(4,128)(2,1)} %broadcast_in_dim.90), calls=%async_computation.3 | async-start | bytes 32768 | tf_op jit(solution)/shard_map/all_to_all | solution.py:126
  27.0 1.8 copy.82
  28.8 1.9 reshape.137
  30.6 1.7 copy.85
  32.3 3.8 copy.110
  36.1 4.0 %copy.80 = bf16[2,32,96,3,128]{4,2,3,1,0:T(8,128)(2,1)} copy(bf16[2,32,96,3,128]{4,1,2,3,0:T(8,128)(2,1)S(1)} %bitcast.291) | data formatting | bytes 9437184 | tf_op jit(solution)/shard_map/transpose | solution.py:65
  42.2 6.2 %all-to-all-start.7 = ((bf16[32,32,128]{2,1,0:T(8,128)(2,1)}), bf16[32,32,128]{2,1,0:T(8,128)(2,1)S(1)}, u32[]{:S(2)}, u32[]{:S(2)}) async-start(bf16[32,32,128]{2,1,0:T(8,128)(2,1)} %bitcast.53), calls=%async_computation.7 | async-start | bytes 524288 | tf_op jit(solution)/shard_map/all_to_all | solution.py:130
  49.3 7.1 %all-to-all-done.7 = bf16[32,32,128]{2,1,0:T(8,128)(2,1)S(1)} async-done(((bf16[32,32,128]{2,1,0:T(8,128)(2,1)}), bf16[32,32,128]{2,1,0:T(8,128)(2,1)S(1)}, u32[]{:S(2)}, u32[]{:S(2)}) %all-to-all-start.7) | async-done | bytes 262176 | tf_op jit(solution)/shard_map/all_to_all | solution.py:130
  56.4 5.6 %all-to-all-start.6 = ((bf16[32,32,3,128]{3,1,2,0:T(8,128)(2,1)}), bf16[32,32,3,128]{3,1,2,0:T(8,128)(2,1)S(1)}, u32[]{:S(2)}, u32[]{:S(2)}) async-start(bf16[32,32,3,128]{3,1,2,0:T(8,128)(2,1)} %bitcast.48), calls=%async_computation.6 | async-start | bytes 1572864 | tf_op jit(solution)/shard_map/all_to_all | solution.py:129
  63.2 2.9 collective-permute-start.6
  67.1 2.2 collective-permute-start.7
  71.5 2.2 collective-permute-start.9
  74.6 4.0 %collective-permute-done.5 = bf16[2,96,2,128]{3,1,2,0:T(8,128)(2,1)S(1)} collective-permute-done((bf16[2,96,2,128]{3,1,2,0:T(8,128)(2,1)}, bf16[2,96,2,128]{3,1,2,0:T(8,128)(2,1)S(1)}, u32[]{:S(2)}, u32[]{:S(2)}) %collective-permute-start.5) | collective-permute-done | bytes 98336 | tf_op jit(solution)/shard_map/ppermute | solution.py:29
  78.6 2.9 collective-permute-start.10
  82.1 12.7 %all-to-all-start.2 = ((bf16[64,32,2,128]{3,1,2,0:T(8,128)(2,1)}), bf16[64,32,2,128]{3,1,2,0:T(8,128)(2,1)}, u32[]{:S(2)}, u32[]{:S(2)}) async-start(bf16[64,32,2,128]{3,1,2,0:T(8,128)(2,1)} %bitcast.36), calls=%async_computation.2 | async-start | bytes 2097152 | tf_op jit(solution)/shard_map/all_to_all | solution.py:125
  94.8 1.2 collective-permute-start.11
  98.7 1.3 collective-permute-start.13
  101.0 1.3 collective-permute-start.14
  104.0 27.0 %collective-permute-done.11 = bf16[2,96,2,128]{3,1,2,0:T(8,128)(2,1)S(1)} collective-permute-done((bf16[2,96,2,128]{3,1,2,0:T(8,128)(2,1)S(1)}, bf16[2,96,2,128]{3,1,2,0:T(8,128)(2,1)S(1)}, u32[]{:S(2)}, u32[]{:S(2)}) %collective-permute-start.11) | collective-permute-done | bytes 98336 | tf_op jit(solution)/shard_map/ppermute | solution.py:29
  131.1 3.0 collective-permute-done.12
  135.3 2.3 collective-permute-done.14
  139.4 4.1 %all-to-all-start.1 = ((bf16[64,96,128]{2,1,0:T(8,128)(2,1)}), bf16[64,96,128]{2,1,0:T(8,128)(2,1)S(1)}, u32[]{:S(2)}, u32[]{:S(2)}) async-start(bf16[64,96,128]{2,1,0:T(8,128)(2,1)} %bitcast.30), calls=%async_computation.1 | async-start | bytes 3145728 | tf_op jit(solution)/shard_map/all_to_all | solution.py:124
  144.3 6.3 %while.73 = (s32[]{:T(128)}, bf16[2,512,128]{2,1,0:T(8,128)(2,1)}, bf16[2,512,128]{2,1,0:T(8,128)(2,1)S(1)}, bf16[2,1536,2,128]{3,1,2,0:T(8,128)(2,1)S(1)}, s32[]{:T(128)}) while((s32[]{:T(128)}, bf16[2,512,128]{2,1,0:T(8,128)(2,1)}, bf16[2,512,128]{2,1,0:T(8,128)(2,1)S(1)}, bf16[2,1536,2,128]{3,1,2,0:T(8,128)(2,1)S(1)}, s32[]{:T(128)}) %tuple.156), condition=%wide.region_19.20_spmd, body=%wide.region_16.19_spmd.sunk | while | flops 408222720 | bytes 14166153 | solution.py:137
  150.6 1.2 copy.94
  151.8 2.1 while.72
  155.0 2.3 copy.86
  157.3 22.4 %all-to-all-done.1 = bf16[64,96,128]{2,1,0:T(8,128)(2,1)S(1)} async-done(((bf16[64,96,128]{2,1,0:T(8,128)(2,1)}), bf16[64,96,128]{2,1,0:T(8,128)(2,1)S(1)}, u32[]{:S(2)}, u32[]{:S(2)}) %all-to-all-start.1) | async-done | bytes 1572896 | tf_op jit(solution)/shard_map/all_to_all | solution.py:124
  179.7 5.5 %all-to-all-start = ((bf16[64,96,3,128]{3,1,2,0:T(8,128)(2,1)}), bf16[64,96,3,128]{3,1,2,0:T(8,128)(2,1)}, u32[]{:S(2)}, u32[]{:S(2)}) async-start(bf16[64,96,3,128]{3,1,2,0:T(8,128)(2,1)} %bitcast.290), calls=%async_computation | async-start | bytes 9437184 | tf_op jit(solution)/shard_map/all_to_all | solution.py:123
  185.4 1.3 broadcast.85.clone
  186.7 17.0 %while.71 = (s32[]{:T(128)}, bf16[4,1536,128]{2,1,0:T(8,128)(2,1)}, bf16[4,1536,128]{2,1,0:T(8,128)(2,1)S(1)}, bf16[4,512,2,128]{3,1,2,0:T(8,128)(2,1)}, bf16[4,...) while((s32[]{:T(128)}, bf16[4,1536,128]{2,1,0:T(8,128)(2,1)}, ...), condition=%wide.region_11.12_spmd, body=%wide.region_6.11_spmd.sunk | while | flops 204570624 | bytes 8015114 | solution.py:135
  187.8 2.4 while.75
  192.0 2.4 while.75
  196.3 2.4 while.75
  200.5 2.4 while.75
  203.7 85.3 %all-to-all-done = bf16[64,96,3,128]{3,1,2,0:T(8,128)(2,1)} async-done(((bf16[64,96,3,128]{3,1,2,0:T(8,128)(2,1)}), bf16[64,96,3,128]{3,1,2,0:T(8,128)(2,1)}, u32[]{:S(2)}, u32[]{:S(2)}) %all-to-all-start) | async-done | bytes 4718624 | tf_op jit(solution)/shard_map/all_to_all | solution.py:123
  288.9 4.9 %all-to-all-start.8 = ((bf16[2,512,128]{2,0,1:T(2,128)(2,1)}), bf16[2,512,128]{2,0,1:T(2,128)(2,1)}, u32[]{:S(2)}, u32[]{:S(2)}) async-start(bf16[2,512,128]{2,0,1:T(2,128)(2,1)} %copy.100), calls=%async_computation.8 | async-start | bytes 524288 | tf_op jit(solution)/shard_map/all_to_all | solution.py:153
  293.9 5.6 %copy.81 = bf16[4,16,96,3,128]{4,2,1,3,0:T(8,128)(2,1)} copy(bf16[4,16,96,3,128]{4,2,3,0,1:T(8,128)(2,1)} %bitcast.27) | data formatting | bytes 9437184 | tf_op jit(solution)/shard_map/all_to_all | solution.py:123
  299.7 29.7 %while.69 = (s32[]{:T(128)}, bf16[4,1536,128]{2,1,0:T(8,128)(2,1)S(1)}, bf16[4,1536,3,128]{3,1,2,0:T(8,128)(2,1)}, s32[]{:T(128)}, s32[]{:T(128)}, /*index=5*/s32[]{:T(128)}) while((s32[]{:T(128)}, bf16[4,1536,128]{2,1,0:T(8,128)(2,1)S(1)}, bf16[4,1536,3,128]{3,1,2,0:T(8,128)(2,1)}, s32[]{:T(128)}, s32[]{:T(128)}, /*index=5*/s32[]{:T(128)}) %tuple.151), condition=%wide.region_5.6_spmd, body=%wide.region_0.5_spmd.sunk | while | flops 614693376 | bytes 20858080 | solution.py:134
  299.7 1.4 dynamic-slice_bitcast_fusion.23
  301.1 5.9 %while.74 = (s32[]{:T(128)}, bf16[2,768,128]{2,1,0:T(8,128)(2,1)S(1)}, bf16[2,768,128]{2,1,0:T(8,128)(2,1)S(1)}, bf16[1536,128]{1,0:T(8,128)(2,1)S(1)}, bf16[1536,128]{1,0:T(8,128)(2,1)S(1)}, /*index=5*/s32[]{:T(128)}) while((s32[]{:T(128)}, bf16[2,768,128]{2,1,0:T(8,128)(2,1)S(1)}, bf16[2,768,128]{2,1,0:T(8,128)(2,1)S(1)}, ...), condition=%wide.region_4.4_spmd, body=%wide.region_1.3_spmd.sunk | while | flops 614693376 | bytes 15352917 | solution.py:55
  302.9 1.2 fusion.71
  305.8 1.2 fusion.71
  307.1 1.4 dynamic-slice_bitcast_fusion.23
  308.6 5.9 %while.74 = (s32[]{:T(128)}, bf16[2,768,128]{2,1,0:T(8,128)(2,1)S(1)}, bf16[2,768,128]{2,1,0:T(8,128)(2,1)S(1)}, bf16[1536,128]{1,0:T(8,128)(2,1)S(1)}, bf16[1536,128]{1,0:T(8,128)(2,1)S(1)}, /*index=5*/s32[]{:T(128)}) while((s32[]{:T(128)}, bf16[2,768,128]{2,1,0:T(8,128)(2,1)S(1)}, bf16[2,768,128]{2,1,0:T(8,128)(2,1)S(1)}, ...), condition=%wide.region_4.4_spmd, body=%wide.region_1.3_spmd.sunk | while | flops 614693376 | bytes 15352917 | solution.py:55
  310.3 1.2 fusion.71
  314.5 1.4 dynamic-slice_bitcast_fusion.23
  316.0 5.9 %while.74 = (s32[]{:T(128)}, bf16[2,768,128]{2,1,0:T(8,128)(2,1)S(1)}, bf16[2,768,128]{2,1,0:T(8,128)(2,1)S(1)}, bf16[1536,128]{1,0:T(8,128)(2,1)S(1)}, bf16[1536,128]{1,0:T(8,128)(2,1)S(1)}, /*index=5*/s32[]{:T(128)}) while((s32[]{:T(128)}, bf16[2,768,128]{2,1,0:T(8,128)(2,1)S(1)}, bf16[2,768,128]{2,1,0:T(8,128)(2,1)S(1)}, ...), condition=%wide.region_4.4_spmd, body=%wide.region_1.3_spmd.sunk | while | flops 614693376 | bytes 15352917 | solution.py:55
  317.8 1.2 fusion.71
  320.7 1.2 fusion.71
  322.0 1.4 dynamic-slice_bitcast_fusion.23
  323.4 5.9 %while.74 = (s32[]{:T(128)}, bf16[2,768,128]{2,1,0:T(8,128)(2,1)S(1)}, bf16[2,768,128]{2,1,0:T(8,128)(2,1)S(1)}, bf16[1536,128]{1,0:T(8,128)(2,1)S(1)}, bf16[1536,128]{1,0:T(8,128)(2,1)S(1)}, /*index=5*/s32[]{:T(128)}) while((s32[]{:T(128)}, bf16[2,768,128]{2,1,0:T(8,128)(2,1)S(1)}, bf16[2,768,128]{2,1,0:T(8,128)(2,1)S(1)}, ...), condition=%wide.region_4.4_spmd, body=%wide.region_1.3_spmd.sunk | while | flops 614693376 | bytes 15352917 | solution.py:55
  325.2 1.2 fusion.71
  328.1 1.2 fusion.71
  329.4 1.9 add_convert_fusion
  331.3 8.2 %copy.88 = bf16[4,1536,128]{2,0,1:T(4,128)(2,1)} copy(bf16[4,1536,128]{2,1,0:T(8,128)(2,1)S(1)} %add_convert_fusion) | data formatting | bytes 3145728 | tf_op jit(solution)/shard_map/convert_element_type | solution.py:147
  339.5 6.0 %all-to-all-start.4 = ((bf16[4,1536,128]{2,0,1:T(4,128)(2,1)}), bf16[4,1536,128]{2,0,1:T(4,128)(2,1)S(1)}, u32[]{:S(2)}, u32[]{:S(2)}) async-start(bf16[4,1536,128]{2,0,1:T(4,128)(2,1)} %copy.88), calls=%async_computation.4 | async-start | bytes 3145728 | tf_op jit(solution)/shard_map/all_to_all | solution.py:152
  347.3 34.4 %all-to-all-done.4 = bf16[4,1536,128]{2,0,1:T(4,128)(2,1)S(1)} async-done(((bf16[4,1536,128]{2,0,1:T(4,128)(2,1)}), bf16[4,1536,128]{2,0,1:T(4,128)(2,1)S(1)}, u32[]{:S(2)}, u32[]{:S(2)}) %all-to-all-start.4) | async-done | bytes 1572896 | tf_op jit(solution)/shard_map/all_to_all | solution.py:152
  382.1 1.6 copy.116
  (218 shorter events, 67.2 us)
Async XLA Ops:
  0.6 26.1 %copy-start = (f32[4,4096]{1,0:T(4,128)S(1)}, f32[4,4096]{1,0:T(4,128)}, u32[]{:S(2)}) copy-start(f32[4,4096]{1,0:T(4,128)} %param.30) | copy-start | bytes 196612
  4.2 5.5 %copy-start.21 = (s32[2]{0:T(128)S(1)}, s32[2]{0:T(128)}, u32[]{:S(2)}) copy-start(s32[2]{0:T(128)} %param.28) | copy-start | bytes 28
  5.6 56.6 %collective-permute-start = (bf16[2,96,2,128]{3,1,2,0:T(8,128)(2,1)}, bf16[2,96,2,128]{3,1,2,0:T(8,128)(2,1)}, u32[]{:S(2)}, u32[]{:S(2)}) collective-permute-start(bf16[2,96,2,128]{3,1,2,0:T(8,128)(2,1)} %get-tuple-element.267), channel_id=1, source_target_pairs={{0,1},{1,0},{2,3},{3,2},{4,5},{5,4},{6,7},{7,6},{8,9},{9,8},{10,11... | collective-permute-start | bytes 294920 | tf_op jit(solution)/shard_map/ppermute | solution.py:29
  6.2 57.0 %collective-permute-start.1 = (bf16[2,96,2,128]{3,1,2,0:T(8,128)(2,1)}, bf16[2,96,2,128]{3,1,2,0:T(8,128)(2,1)}, u32[]{:S(2)}, u32[]{:S(2)}) collective-permute-start(bf16[2,96,2,128]{3,1,2,0:T(8,128)(2,1)} %get-tuple-element.266), channel_id=1, source_target_pairs={{0,2},{1,3},{2,0},{3,1},{4,6},{5,7},{6,4},{7,5},{8,10},{9,11},{10,... | collective-permute-start | bytes 294920 | tf_op jit(solution)/shard_map/ppermute | solution.py:29
  6.5 60.6 %collective-permute-start.2 = (bf16[2,96,2,128]{3,1,2,0:T(8,128)(2,1)}, bf16[2,96,2,128]{3,1,2,0:T(8,128)(2,1)}, u32[]{:S(2)}, u32[]{:S(2)}) collective-permute-start(bf16[2,96,2,128]{3,1,2,0:T(8,128)(2,1)} %get-tuple-element.265), channel_id=1, source_target_pairs={{0,3},{1,2},{2,1},{3,0},{4,7},{5,6},{6,5},{7,4},{8,11},{9,10},{10,... | collective-permute-start | bytes 294920 | tf_op jit(solution)/shard_map/ppermute | solution.py:29
  7.9 62.3 %collective-permute-start.3 = (bf16[2,96,2,128]{3,1,2,0:T(8,128)(2,1)}, bf16[2,96,2,128]{3,1,2,0:T(8,128)(2,1)}, u32[]{:S(2)}, u32[]{:S(2)}) collective-permute-start(bf16[2,96,2,128]{3,1,2,0:T(8,128)(2,1)} %get-tuple-element.264), channel_id=1, source_target_pairs={{0,4},{1,5},{2,6},{3,7},{4,0},{5,1},{6,2},{7,3},{8,12},{9,13},{10,... | collective-permute-start | bytes 294920 | tf_op jit(solution)/shard_map/ppermute | solution.py:29
  8.1 63.4 %collective-permute-start.4 = (bf16[2,96,2,128]{3,1,2,0:T(8,128)(2,1)}, bf16[2,96,2,128]{3,1,2,0:T(8,128)(2,1)}, u32[]{:S(2)}, u32[]{:S(2)}) collective-permute-start(bf16[2,96,2,128]{3,1,2,0:T(8,128)(2,1)} %get-tuple-element.263), channel_id=1, source_target_pairs={{0,5},{1,4},{2,7},{3,6},{4,1},{5,0},{6,3},{7,2},{8,13},{9,12},{10,... | collective-permute-start | bytes 294920 | tf_op jit(solution)/shard_map/ppermute | solution.py:29
  10.4 9.7 %all-to-all-start.5 = ((bf16[16,2,32]{2,1,0:T(2,128)(2,1)}), bf16[16,2,32]{2,1,0:T(2,128)(2,1)S(1)}, u32[]{:S(2)}, u32[]{:S(2)}) async-start(bf16[16,2,32]{2,1,0:T(2,128)(2,1)} %broadcast_in_dim.91), calls=%async_computation.5 | async-start | bytes 16384 | tf_op jit(solution)/shard_map/all_to_all | solution.py:132
  18.2 1.0 copy-start.9
  18.2 8.6 %copy-start.19 = (s32[2]{0:T(128)S(1)}, s32[2]{0:T(128)}, u32[]{:S(2)}) copy-start(s32[2]{0:T(128)} %param.29) | copy-start | bytes 28
  20.7 21.4 %all-to-all-start.3 = ((bf16[16,4,32]{2,1,0:T(4,128)(2,1)}), bf16[16,4,32]{2,1,0:T(4,128)(2,1)S(1)}, u32[]{:S(2)}, u32[]{:S(2)}) async-start(bf16[16,4,32]{2,1,0:T(4,128)(2,1)} %broadcast_in_dim.90), calls=%async_computation.3 | async-start | bytes 32768 | tf_op jit(solution)/shard_map/all_to_all | solution.py:126
  36.1 4.8 %copy-start.8 = (bf16[2,32,3,2048]{3,1,2,0:T(8,128)(2,1)S(1)}, bf16[2,32,3,2048]{3,1,2,0:T(8,128)(2,1)}, u32[]{:S(2)}) copy-start(bf16[2,32,3,2048]{3,1,2,0:T(8,128)(2,1)} %param.25) | copy-start | bytes 2359300
  40.9 7.5 %copy-start.20 = (f32[4,2048]{1,0:T(4,128)S(1)}, f32[4,2048]{1,0:T(4,128)}, u32[]{:S(2)}) copy-start(f32[4,2048]{1,0:T(4,128)} %param.31) | copy-start | bytes 98308
  42.2 24.9 %copy-start.17 = (bf16[2,96,2,128]{3,1,2,0:T(8,128)(2,1)S(1)}, bf16[2,96,2,128]{3,1,2,0:T(8,128)(2,1)}, u32[]{:S(2)}) copy-start(bf16[2,96,2,128]{3,1,2,0:T(8,128)(2,1)} %get-tuple-element.260) | copy-start | bytes 294916
  42.2 28.0 %copy-start.16 = (bf16[2,96,2,128]{3,1,2,0:T(8,128)(2,1)S(1)}, bf16[2,96,2,128]{3,1,2,0:T(8,128)(2,1)}, u32[]{:S(2)}) copy-start(bf16[2,96,2,128]{3,1,2,0:T(8,128)(2,1)} %get-tuple-element.259) | copy-start | bytes 294916
  42.2 29.3 %copy-start.15 = (bf16[2,96,2,128]{3,1,2,0:T(8,128)(2,1)S(1)}, bf16[2,96,2,128]{3,1,2,0:T(8,128)(2,1)}, u32[]{:S(2)}) copy-start(bf16[2,96,2,128]{3,1,2,0:T(8,128)(2,1)} %get-tuple-element.258) | copy-start | bytes 294916
  42.2 36.4 %copy-start.14 = (bf16[2,96,2,128]{3,1,2,0:T(8,128)(2,1)S(1)}, bf16[2,96,2,128]{3,1,2,0:T(8,128)(2,1)}, u32[]{:S(2)}) copy-start(bf16[2,96,2,128]{3,1,2,0:T(8,128)(2,1)} %get-tuple-element.257) | copy-start | bytes 294916
  42.2 14.2 %all-to-all-start.7 = ((bf16[32,32,128]{2,1,0:T(8,128)(2,1)}), bf16[32,32,128]{2,1,0:T(8,128)(2,1)S(1)}, u32[]{:S(2)}, u32[]{:S(2)}) async-start(bf16[32,32,128]{2,1,0:T(8,128)(2,1)} %bitcast.53), calls=%async_computation.7 | async-start | bytes 524288 | tf_op jit(solution)/shard_map/all_to_all | solution.py:130
  56.4 25.7 %copy-start.3 = (bf16[32,32,128]{2,1,0:T(8,128)(2,1)}, bf16[32,32,128]{2,1,0:T(8,128)(2,1)S(1)}, u32[]{:S(2)}) copy-start(bf16[32,32,128]{2,1,0:T(8,128)(2,1)S(1)} %all-to-all-done.7) | copy-start | bytes 786436
  56.4 25.7 %all-to-all-start.6 = ((bf16[32,32,3,128]{3,1,2,0:T(8,128)(2,1)}), bf16[32,32,3,128]{3,1,2,0:T(8,128)(2,1)S(1)}, u32[]{:S(2)}, u32[]{:S(2)}) async-start(bf16[32,32,3,128]{3,1,2,0:T(8,128)(2,1)} %bitcast.48), calls=%async_computation.6 | async-start | bytes 1572864 | tf_op jit(solution)/shard_map/all_to_all | solution.py:129
  62.2 16.4 %collective-permute-start.5 = (bf16[2,96,2,128]{3,1,2,0:T(8,128)(2,1)}, bf16[2,96,2,128]{3,1,2,0:T(8,128)(2,1)S(1)}, u32[]{:S(2)}, u32[]{:S(2)}) collective-permute-start(bf16[2,96,2,128]{3,1,2,0:T(8,128)(2,1)} %get-tuple-element.262), channel_id=1, source_target_pairs={{0,6},{1,7},{2,4},{3,5},{4,2},{5,3},{6,0},{7,1},{8,14},{9,15},{10,... | collective-permute-start | bytes 294920 | tf_op jit(solution)/shard_map/ppermute | solution.py:29
  63.2 31.6 %copy-start.13 = (bf16[2,96,2,128]{3,1,2,0:T(8,128)(2,1)S(1)}, bf16[2,96,2,128]{3,1,2,0:T(8,128)(2,1)}, u32[]{:S(2)}) copy-start(bf16[2,96,2,128]{3,1,2,0:T(8,128)(2,1)} %get-tuple-element.256) | copy-start | bytes 294916
  63.2 31.5 %collective-permute-start.6 = (bf16[2,96,2,128]{3,1,2,0:T(8,128)(2,1)}, bf16[2,96,2,128]{3,1,2,0:T(8,128)(2,1)}, u32[]{:S(2)}, u32[]{:S(2)}) collective-permute-start(bf16[2,96,2,128]{3,1,2,0:T(8,128)(2,1)} %get-tuple-element.261), channel_id=1, source_target_pairs={{0,7},{1,6},{2,5},{3,4},{4,3},{5,2},{6,1},{7,0},{8,15},{9,14},{10,... | collective-permute-start | bytes 294920 | tf_op jit(solution)/shard_map/ppermute | solution.py:29
  67.0 29.9 %copy-start.12 = (bf16[2,96,2,128]{3,1,2,0:T(8,128)(2,1)S(1)}, bf16[2,96,2,128]{3,1,2,0:T(8,128)(2,1)}, u32[]{:S(2)}) copy-start(bf16[2,96,2,128]{3,1,2,0:T(8,128)(2,1)} %get-tuple-element.255) | copy-start | bytes 294916
  67.1 29.9 %collective-permute-start.7 = (bf16[2,96,2,128]{3,1,2,0:T(8,128)(2,1)S(1)}, bf16[2,96,2,128]{3,1,2,0:T(8,128)(2,1)}, u32[]{:S(2)}, u32[]{:S(2)}) collective-permute-start(bf16[2,96,2,128]{3,1,2,0:T(8,128)(2,1)S(1)} %copy-done.17), channel_id=1, source_target_pairs={{0,8},{1,9},{2,10},{3,11},{4,12},{5,13},{6,14},{7,15},{8,0},{9,1},... | collective-permute-start | bytes 294920 | tf_op jit(solution)/shard_map/ppermute | solution.py:29
  70.2 28.6 %copy-start.11 = (bf16[2,96,2,128]{3,1,2,0:T(8,128)(2,1)S(1)}, bf16[2,96,2,128]{3,1,2,0:T(8,128)(2,1)}, u32[]{:S(2)}) copy-start(bf16[2,96,2,128]{3,1,2,0:T(8,128)(2,1)} %get-tuple-element.254) | copy-start | bytes 294916
  70.2 28.5 %collective-permute-start.8 = (bf16[2,96,2,128]{3,1,2,0:T(8,128)(2,1)S(1)}, bf16[2,96,2,128]{3,1,2,0:T(8,128)(2,1)}, u32[]{:S(2)}, u32[]{:S(2)}) collective-permute-start(bf16[2,96,2,128]{3,1,2,0:T(8,128)(2,1)S(1)} %copy-done.16), channel_id=1, source_target_pairs={{0,9},{1,8},{2,11},{3,10},{4,13},{5,12},{6,15},{7,14},{8,1},{9,0},... | collective-permute-start | bytes 294920 | tf_op jit(solution)/shard_map/ppermute | solution.py:29
  71.5 29.5 %copy-start.10 = (bf16[2,96,2,128]{3,1,2,0:T(8,128)(2,1)S(1)}, bf16[2,96,2,128]{3,1,2,0:T(8,128)(2,1)}, u32[]{:S(2)}) copy-start(bf16[2,96,2,128]{3,1,2,0:T(8,128)(2,1)} %get-tuple-element.253) | copy-start | bytes 294916
  71.5 29.5 %collective-permute-start.9 = (bf16[2,96,2,128]{3,1,2,0:T(8,128)(2,1)S(1)}, bf16[2,96,2,128]{3,1,2,0:T(8,128)(2,1)}, u32[]{:S(2)}, u32[]{:S(2)}) collective-permute-start(bf16[2,96,2,128]{3,1,2,0:T(8,128)(2,1)S(1)} %copy-done.15), channel_id=1, source_target_pairs={{0,10},{1,11},{2,8},{3,9},{4,14},{5,15},{6,12},{7,13},{8,2},{9,3},... | collective-permute-start | bytes 294920 | tf_op jit(solution)/shard_map/ppermute | solution.py:29
  78.6 24.5 %collective-permute-start.10 = (bf16[2,96,2,128]{3,1,2,0:T(8,128)(2,1)S(1)}, bf16[2,96,2,128]{3,1,2,0:T(8,128)(2,1)}, u32[]{:S(2)}, u32[]{:S(2)}) collective-permute-start(bf16[2,96,2,128]{3,1,2,0:T(8,128)(2,1)S(1)} %copy-done.14), channel_id=1, source_target_pairs={{0,11},{1,10},{2,9},{3,8},{4,15},{5,14},{6,13},{7,12},{8,3},{9,2},... | collective-permute-start | bytes 294920 | tf_op jit(solution)/shard_map/ppermute | solution.py:29
  82.1 49.0 %copy-start.2 = (bf16[32,32,3,128]{3,1,2,0:T(8,128)(2,1)}, bf16[32,32,3,128]{3,1,2,0:T(8,128)(2,1)S(1)}, u32[]{:S(2)}) copy-start(bf16[32,32,3,128]{3,1,2,0:T(8,128)(2,1)S(1)} %all-to-all-done.6) | copy-start | bytes 2359300
  82.1 57.3 %all-to-all-start.2 = ((bf16[64,32,2,128]{3,1,2,0:T(8,128)(2,1)}), bf16[64,32,2,128]{3,1,2,0:T(8,128)(2,1)}, u32[]{:S(2)}, u32[]{:S(2)}) async-start(bf16[64,32,2,128]{3,1,2,0:T(8,128)(2,1)} %bitcast.36), calls=%async_computation.2 | async-start | bytes 2097152 | tf_op jit(solution)/shard_map/all_to_all | solution.py:125
  94.8 36.3 %collective-permute-start.11 = (bf16[2,96,2,128]{3,1,2,0:T(8,128)(2,1)S(1)}, bf16[2,96,2,128]{3,1,2,0:T(8,128)(2,1)S(1)}, u32[]{:S(2)}, u32[]{:S(2)}) collective-permute-start(bf16[2,96,2,128]{3,1,2,0:T(8,128)(2,1)S(1)} %copy-done.13), channel_id=1, source_target_pairs={{0,12},{1,13},{2,14},{3,15},{4,8},{5,9},{6,10},{7,11},{8,4},{9,5},... | collective-permute-start | bytes 294920 | tf_op jit(solution)/shard_map/ppermute | solution.py:29
  96.9 37.2 %collective-permute-start.12 = (bf16[2,96,2,128]{3,1,2,0:T(8,128)(2,1)S(1)}, bf16[2,96,2,128]{3,1,2,0:T(8,128)(2,1)S(1)}, u32[]{:S(2)}, u32[]{:S(2)}) collective-permute-start(bf16[2,96,2,128]{3,1,2,0:T(8,128)(2,1)S(1)} %copy-done.12), channel_id=1, source_target_pairs={{0,13},{1,12},{2,15},{3,14},{4,9},{5,8},{6,11},{7,10},{8,5},{9,4},... | collective-permute-start | bytes 294920 | tf_op jit(solution)/shard_map/ppermute | solution.py:29
  98.7 36.5 %collective-permute-start.13 = (bf16[2,96,2,128]{3,1,2,0:T(8,128)(2,1)S(1)}, bf16[2,96,2,128]{3,1,2,0:T(8,128)(2,1)S(1)}, u32[]{:S(2)}, u32[]{:S(2)}) collective-permute-start(bf16[2,96,2,128]{3,1,2,0:T(8,128)(2,1)S(1)} %copy-done.11), channel_id=1, source_target_pairs={{0,14},{1,15},{2,12},{3,13},{4,10},{5,11},{6,8},{7,9},{8,6},{9,7},... | collective-permute-start | bytes 294920 | tf_op jit(solution)/shard_map/ppermute | solution.py:29
  101.0 36.6 %collective-permute-start.14 = (bf16[2,96,2,128]{3,1,2,0:T(8,128)(2,1)S(1)}, bf16[2,96,2,128]{3,1,2,0:T(8,128)(2,1)S(1)}, u32[]{:S(2)}, u32[]{:S(2)}) collective-permute-start(bf16[2,96,2,128]{3,1,2,0:T(8,128)(2,1)S(1)} %copy-done.10), channel_id=1, source_target_pairs={{0,15},{1,14},{2,13},{3,12},{4,11},{5,10},{6,9},{7,8},{8,7},{9,6},... | collective-permute-start | bytes 294920 | tf_op jit(solution)/shard_map/ppermute | solution.py:29
  138.4 1.0 copy-start.4
  139.4 40.3 %all-to-all-start.1 = ((bf16[64,96,128]{2,1,0:T(8,128)(2,1)}), bf16[64,96,128]{2,1,0:T(8,128)(2,1)S(1)}, u32[]{:S(2)}, u32[]{:S(2)}) async-start(bf16[64,96,128]{2,1,0:T(8,128)(2,1)} %bitcast.30), calls=%async_computation.1 | async-start | bytes 3145728 | tf_op jit(solution)/shard_map/all_to_all | solution.py:124
  145.0 1.0 copy-start.5
  146.7 0.7 copy-start.6
  148.1 1.0 copy-start.5
  149.9 0.7 copy-start.6
  151.8 2.1 copy-start.7
  179.7 109.2 %all-to-all-start = ((bf16[64,96,3,128]{3,1,2,0:T(8,128)(2,1)}), bf16[64,96,3,128]{3,1,2,0:T(8,128)(2,1)}, u32[]{:S(2)}, u32[]{:S(2)}) async-start(bf16[64,96,3,128]{3,1,2,0:T(8,128)(2,1)} %bitcast.290), calls=%async_computation | async-start | bytes 9437184 | tf_op jit(solution)/shard_map/all_to_all | solution.py:123
  288.9 50.6 %all-to-all-start.8 = ((bf16[2,512,128]{2,0,1:T(2,128)(2,1)}), bf16[2,512,128]{2,0,1:T(2,128)(2,1)}, u32[]{:S(2)}, u32[]{:S(2)}) async-start(bf16[2,512,128]{2,0,1:T(2,128)(2,1)} %copy.100), calls=%async_computation.8 | async-start | bytes 524288 | tf_op jit(solution)/shard_map/all_to_all | solution.py:153
  299.7 29.7 %copy-start.18 = (f32[4,128]{1,0:T(4,128)S(1)}, f32[4,128]{1,0:T(4,128)}, u32[]{:S(2)}) copy-start(f32[4,128]{1,0:T(4,128)} %constant_dynamic-slice_fusion.2) | copy-start | bytes 6148
  339.5 42.2 %all-to-all-start.4 = ((bf16[4,1536,128]{2,0,1:T(4,128)(2,1)}), bf16[4,1536,128]{2,0,1:T(4,128)(2,1)S(1)}, u32[]{:S(2)}, u32[]{:S(2)}) async-start(bf16[4,1536,128]{2,0,1:T(4,128)(2,1)} %copy.88), calls=%async_computation.4 | async-start | bytes 3145728 | tf_op jit(solution)/shard_map/all_to_all | solution.py:152
  382.1 1.6 copy-start.1
